TPU v7x, 128 devices: a whole 4x4x4 slice. The times are simulated.
128 devices in a mesh: dp: 8 (over y, z_hi), mp: 16 (over z_lo, x, core).
Axes of the slice: x: 4, y: 4, z: 4 (z_hi: 2, z_lo: 2; z = z_hi * 2 + z_lo), core: 2. Of those that a mesh axis runs over, the one named last changes fastest.
Arguments:
- grad: bfloat16 [8192, 16384], P(('dp', 'mp')), as said below
- block_owner: int32 [128], replicated, may hold values from 0 to 127, as said below
- left_stat: float32 [128, 1024, 1024], P(('dp', 'mp')), as said below
- right_stat: float32 [128, 1024, 1024], P(('dp', 'mp')), as said below
- left_root: bfloat16 [128, 1024, 1024], P(('dp', 'mp'))
- right_root: bfloat16 [128, 1024, 1024], P(('dp', 'mp'))
Outputs:
- new_left: float32 [128, 1024, 1024], P(('dp', 'mp'))
- new_right: float32 [128, 1024, 1024], P(('dp', 'mp'))
- update: bfloat16 [8192, 16384], P(('dp', 'mp'))
Inputs may be any that keep to these rules, and one draw needn't show every extreme that they name: `block_owner`: A permutation: each device owns exactly one block, and of each band's 16 blocks exactly 2 are owned by devices of each dp index (owner = dp index * 16 + mp index). `grad`: gradient entries, scaled per row and per column. `left_stat`: symmetric positive definite. `right_stat`: symmetric positive definite.
All inputs are finite; a program needn't handle non-finite values.
Results may differ from a plain program's by a relative error of at most 0.0039.
The roundings to bfloat16 on the way count: a program that leaves them out, or rounds other values in their place, can miss the bound.
Values may be sent and summed in bfloat16 or wider, within the bound.
A program may use at most 256 MiB of HBM per device.

v0:
```python
import functools

import jax
import jax.numpy as jnp
from jax import lax
from jax.sharding import Mesh
from jax.sharding import PartitionSpec as P

BLK = 1024
DP = ("dp_0", "dp_1")
MP = ("mp_0", "mp_1", "mp_2")
DP_MP = ("dp_0", "dp_1", "mp_0", "mp_1", "mp_2")


clip_level = 0.5
beta_stat = 0.95


def by_axis(shard, axes):
    return functools.reduce(lax.psum, axes, shard)


def split_up(shard, dim, devices):
    shape = shard.shape
    parts = shard.reshape(*shape[:dim], devices, shape[dim] // devices, *shape[dim + 1 :])
    return jnp.moveaxis(parts, dim, 0)


def piece_ends(length, count):
    unit = 8 if length >= 8 * count else 1
    return [length // unit * k // count * unit for k in range(1, count)]


def laid_out(parts, dim):
    parts = jnp.moveaxis(parts, 0, dim)
    shape = parts.shape
    return parts.reshape(*shape[:dim], shape[dim] * shape[dim + 1], *shape[dim + 2 :])


def cut_exchange(shard, axis, pieces, split_dim, concat_dim):
    parts = split_up(shard, split_dim, lax.axis_size(axis))
    cut = max(range(1, max(2, parts.ndim - 1)), key=lambda d: parts.shape[d])
    outs = []
    for slab in jnp.split(parts, piece_ends(parts.shape[cut], pieces), axis=cut):
        if slab.size:
            outs.append(lax.all_to_all(slab, axis, split_axis=0, concat_axis=0, tiled=True))
    return laid_out(jnp.concatenate(outs, axis=cut), concat_dim)


def per_device(grad, block_owner, left_stat, right_stat, left_root, right_root):
    dp_count = lax.axis_size(DP)
    mp_count = lax.axis_size(MP)
    devices = dp_count * mp_count
    group_size = mp_count // dp_count
    my_band = lax.axis_index(DP)
    shard_rows = grad.shape[0]
    shard_cols = grad.shape[1]
    table = block_owner.reshape(dp_count, mp_count)
    band_owners = lax.dynamic_index_in_dim(table, my_band, 0, keepdims=False)
    pieces = grad.reshape(shard_rows, mp_count, BLK)
    column_order = jnp.argsort(band_owners)
    outbound = jnp.take(pieces, column_order, axis=1)
    banded = lax.all_to_all(outbound, DP, split_axis=1, concat_axis=1, tiled=True)
    sorted_owners = jnp.sort(table, axis=1)
    local_owners = lax.dynamic_slice_in_dim(
        sorted_owners, my_band * group_size, group_size, 1
    ).reshape(mp_count)
    owner_cols = local_owners % mp_count
    sectioned = jnp.take(banded, jnp.argsort(owner_cols), axis=1)
    arrived = lax.all_to_all(sectioned, MP, split_axis=1, concat_axis=0, tiled=True)
    block = arrived.reshape(BLK, BLK)
    values = block.astype(jnp.float32)
    total = by_axis(jnp.sum(values * values), DP_MP)
    mean_square = total / (shard_rows * shard_cols * devices)
    scale = clip_level / jnp.sqrt(mean_square + 1e-06)
    left_gram = jnp.dot(block, block.T, preferred_element_type=jnp.float32)
    right_gram = jnp.dot(block.T, block, preferred_element_type=jnp.float32)
    factor = (1.0 - beta_stat) * scale * scale / BLK
    left_new = beta_stat * left_stat[0] + factor * left_gram
    right_new = beta_stat * right_stat[0] + factor * right_gram
    partial_left = jnp.dot(left_root[0], block, preferred_element_type=jnp.float32).astype(
        jnp.bfloat16
    )
    update_block = (
        jnp.dot(partial_left, right_root[0], preferred_element_type=jnp.float32) * scale
    ).astype(jnp.bfloat16)
    first_back = lax.all_to_all(
        update_block.reshape(BLK, 1, BLK), MP, split_axis=0, concat_axis=1, tiled=True
    )
    second_send = jnp.take(first_back, owner_cols, axis=1)
    second_back = cut_exchange(second_send, DP, 2, 1, 1)
    mine = jnp.take(second_back, jnp.argsort(column_order), axis=1)
    update = mine.reshape(shard_rows, shard_cols)
    return (left_new[None], right_new[None], update)


def solution(mesh):
    split = Mesh(mesh.devices.reshape(4, 2, 2, 4, 2), ("dp_0", "dp_1", "mp_0", "mp_1", "mp_2"))
    in_specs = (
        P(DP_MP, None),
        P(),
        P(DP_MP, None, None),
        P(DP_MP, None, None),
        P(DP_MP, None, None),
        P(DP_MP, None, None),
    )
    out_specs = (P(DP_MP, None, None), P(DP_MP, None, None), P(DP_MP, None))
    return jax.shard_map(
        per_device, mesh=split, in_specs=in_specs, out_specs=out_specs, check_vma=False
    )
```

profile of v0, /device:TPU:0, one launch (start us, length us, event | category | flops | bytes accessed | tf_op | source)
XLA Modules:
  0.0 235.9 jit_solution(18132220174320135936)
XLA Ops:
  0.6 0.0 copy-start
  0.7 0.9 reshape.45
  1.6 1.2 sort.60
  2.8 3.2 %copy.29 = bf16[8,16,8,1024]{3,2,0,1:T(8,128)(2,1)} copy(bf16[8,16,8,1024]{3,2,1,0:T(8,128)(2,1)} %bitcast.76) | data formatting | bytes 4194304 | tf_op jit(solution)/shard_map/reshape | solution.py:60
  6.0 3.6 %gather_fusion = bf16[16,64,1024]{2,1,0:T(8,128)(2,1)} fusion(bf16[64,16,1024]{2,0,1:T(8,128)(2,1)} %bitcast.75, s32[1024]{0:T(1024)S(1)} %pad_clamp_fusion.3), kind=kCustom, calls=%fused_computation.clone | custom fusion | bytes 4194368 | tf_op jit(solution)/shard_map/jit(_take)/gather | solution.py:62
  9.6 3.2 %select_bitcast_fusion.2 = bf16[64,16,1024]{2,0,1:T(8,128)(2,1)} fusion(bf16[16,64,1024]{2,1,0:T(8,128)(2,1)} %gather_fusion, pred[16]{0:T(512)(128)(4,1)S(1)} %compare_and_fusion.3), kind=kLoop, calls=%fused_computation.19 | loop fusion | flops 1048576 | bytes 4194320 | tf_op jit(solution)/shard_map/jit(_take)/select_n | solution.py:62
  12.7 7.9 %all-to-all-start = ((bf16[64,16,1024]{2,0,1:T(8,128)(2,1)}), bf16[64,16,1024]{2,0,1:T(8,128)(2,1)}, u32[]{:S(2)}, u32[]{:S(2)}) async-start(bf16[64,16,1024]{2,0,1:T(8,128)(2,1)} %select_bitcast_fusion.2), calls=%async_computation | async-start | bytes 4194304 | tf_op jit(solution)/shard_map/all_to_all | solution.py:63
  20.6 0.1 copy.20
  20.7 1.2 sort.63
  21.9 0.7 sort.61
  22.6 0.1 copy.21
  22.7 0.1 reshape.46
  22.8 1.2 sort.62
  24.1 27.8 %all-to-all-done = bf16[64,16,1024]{2,0,1:T(8,128)(2,1)} async-done(((bf16[64,16,1024]{2,0,1:T(8,128)(2,1)}), bf16[64,16,1024]{2,0,1:T(8,128)(2,1)}, u32[]{:S(2)}, u32[]{:S(2)}) %all-to-all-start) | async-done | bytes 2097184 | tf_op jit(solution)/shard_map/all_to_all | solution.py:63
  51.9 3.6 %gather_fusion.1 = bf16[16,64,1024]{2,1,0:T(8,128)(2,1)} fusion(bf16[64,16,1024]{2,0,1:T(8,128)(2,1)} %all-to-all-done, s32[1024]{0:T(1024)S(1)} %pad_clamp_fusion.2), kind=kCustom, calls=%fused_computation.1.clone | custom fusion | bytes 4194368 | tf_op jit(solution)/shard_map/jit(_take)/gather | solution.py:69
  55.5 1.8 select_bitcast_fusion.1
  57.3 32.4 %all_to_all.48 = bf16[64,16,1024]{2,0,1:T(8,128)(2,1)S(1)} all-to-all(bf16[64,16,1024]{2,0,1:T(8,128)(2,1)S(1)} %select_bitcast_fusion.1), channel_id=1, replica_groups=mesh['dp_0'=4,'dp_1'=2,'mp_0'=2,'mp_1'=4,'mp_2'=2] {'mp_0','mp_1','mp_2'}, dimensions={1} | all-to-all | bytes 4194304 | tf_op jit(solution)/shard_map/all_to_all | solution.py:70
  89.7 1.3 copy-done.2
  91.0 1.7 multiply_reduce_fusion
  92.7 8.3 %psum.35 = f32[]{:T(128)} all-reduce(f32[]{:T(128)} %multiply_reduce_fusion), channel_id=1, replica_groups=mesh['dp_0'=4,'dp_1'=2,'mp_0'=2,'mp_1'=4,'mp_2'=2] {'dp_0'}, use_global_device_ids=true, to_apply=%region_4.6 | all-reduce | flops 1 | bytes 8 | tf_op jit(solution)/shard_map/psum | solution.py:20
  101.0 7.1 %psum.36 = f32[]{:T(128)} all-reduce(f32[]{:T(128)} %psum.35), channel_id=1, replica_groups=mesh['dp_0'=4,'dp_1'=2,'mp_0'=2,'mp_1'=4,'mp_2'=2] {'dp_1'}, use_global_device_ids=true, to_apply=%region_5.7 | all-reduce | flops 1 | bytes 8 | tf_op jit(solution)/shard_map/psum | solution.py:20
  108.1 5.5 %psum.37 = f32[]{:T(128)} all-reduce(f32[]{:T(128)} %psum.36), channel_id=1, replica_groups=mesh['dp_0'=4,'dp_1'=2,'mp_0'=2,'mp_1'=4,'mp_2'=2] {'mp_0'}, use_global_device_ids=true, to_apply=%region_6.8 | all-reduce | flops 1 | bytes 8 | tf_op jit(solution)/shard_map/psum | solution.py:20
  113.6 8.6 %psum.38 = f32[]{:T(128)} all-reduce(f32[]{:T(128)} %psum.37), channel_id=1, replica_groups=mesh['dp_0'=4,'dp_1'=2,'mp_0'=2,'mp_1'=4,'mp_2'=2] {'mp_1'}, use_global_device_ids=true, to_apply=%region_7.9 | all-reduce | flops 1 | bytes 8 | tf_op jit(solution)/shard_map/psum | solution.py:20
  122.3 3.1 %psum.39 = f32[]{:T(128)} all-reduce(f32[]{:T(128)} %psum.38), channel_id=1, replica_groups=mesh['dp_0'=4,'dp_1'=2,'mp_0'=2,'mp_1'=4,'mp_2'=2] {'mp_2'}, use_global_device_ids=true, to_apply=%region_8.10 | all-reduce | flops 1 | bytes 8 | tf_op jit(solution)/shard_map/psum | solution.py:20
  126.0 0.0 copy-done
  126.0 8.1 %fusion.8 = bf16[1024,1,1024]{2,0,1:T(8,128)(2,1)} fusion(f32[]{:T(128)S(6)} %div.11, bf16[1,1024,1024]{2,1,0:T(8,128)(2,1)S(1)} %copy-done, bf16[1024,1024]{1,0:T(8,128)(2,1)} %bitcast.71, bf16[1,1024,1024]{2,1,0:T(8,128)(2,1)} %param.12), kind=kOutput, calls=%fused_computation.22 | convolution fusion | flops 4298113024 | bytes 8388612 | tf_op jit(solution)/shard_map/dot_general | solution.py:85
  134.2 0.5 broadcast.112
  134.7 3.9 %reduce.1 = bf16[1024,1024]{1,0:T(8,128)(2,1)S(1)} reduce(bf16[1024,1,1024]{2,0,1:T(8,128)(2,1)} %fusion.8, bf16[]{:T(256)} %broadcast.112), dimensions={1}, to_apply=%copy.23.reduce_sub_computation | reduce | bytes 4194306 | tf_op jit(solution)/shard_map/reshape | solution.py:88
  138.6 2.8 %reshape.98 = bf16[16,2,32768]{2,1,0:T(2,128)(2,1)} reshape(bf16[1024,1024]{1,0:T(8,128)(2,1)S(1)} %reduce.1) | data formatting | bytes 4194304
  141.4 3.7 %all-to-all-start.2 = ((bf16[16,2,32768]{2,1,0:T(2,128)(2,1)}), bf16[16,2,32768]{2,1,0:T(2,128)(2,1)S(1)}, u32[]{:S(2)}, u32[]{:S(2)}) async-start(bf16[16,2,32768]{2,1,0:T(2,128)(2,1)} %reshape.98), calls=%async_computation.2 | async-start | bytes 4194304 | tf_op jit(solution)/shard_map/all_to_all | solution.py:87
  145.1 28.0 %all-to-all-done.2 = bf16[16,2,32768]{2,1,0:T(2,128)(2,1)S(1)} async-done(((bf16[16,2,32768]{2,1,0:T(2,128)(2,1)}), bf16[16,2,32768]{2,1,0:T(2,128)(2,1)S(1)}, u32[]{:S(2)}, u32[]{:S(2)}) %all-to-all-start.2) | async-done | bytes 2097184 | tf_op jit(solution)/shard_map/all_to_all | solution.py:87
  173.1 6.7 %reshape.99 = bf16[1024,1,1024]{2,1,0:T(2,128)(2,1)} reshape(bf16[16,2,32768]{2,1,0:T(2,128)(2,1)S(1)} %all-to-all-done.2) | data formatting | bytes 4194304
  179.8 3.0 %copy.25 = bf16[1024,1,1024]{2,0,1:T(8,128)(2,1)S(1)} copy(bf16[1024,1,1024]{2,1,0:T(2,128)(2,1)} %reshape.99) | data formatting | bytes 4194304
  182.8 2.0 gather_fusion.2
  184.8 1.9 broadcast_select_fusion
  186.7 1.7 fusion.18
  188.3 5.0 %all-to-all-start.3 = ((bf16[8,32,2,1024]{3,1,2,0:T(8,128)(2,1)}), bf16[8,32,2,1024]{3,1,2,0:T(8,128)(2,1)S(1)}, u32[]{:S(2)}, u32[]{:S(2)}) async-start(bf16[8,32,2,1024]{3,1,2,0:T(8,128)(2,1)} %get-tuple-element.15), calls=%async_computation.3 | async-start | bytes 2097152 | tf_op jit(solution)/shard_map/all_to_all | solution.py:46
  193.4 0.0 copy-done.3
  193.4 6.6 %fusion.2 = f32[1,1024,1024]{2,1,0:T(8,128)} fusion(f32[1,1024,1024]{2,1,0:T(8,128)} %param.10, bf16[1024,1024]{1,0:T(8,128)(2,1)S(1)} %bitcast.72, f32[]{:T(128)S(6)} %div.10), kind=kOutput, calls=%fused_computation.8 | convolution fusion | flops 2150629376 | bytes 10485764 | tf_op jit(solution)/shard_map/dot_general | solution.py:76
  200.0 9.2 %all-to-all-done.3 = bf16[8,32,2,1024]{3,1,2,0:T(8,128)(2,1)S(1)} async-done(((bf16[8,32,2,1024]{3,1,2,0:T(8,128)(2,1)}), bf16[8,32,2,1024]{3,1,2,0:T(8,128)(2,1)S(1)}, u32[]{:S(2)}, u32[]{:S(2)}) %all-to-all-start.3) | async-done | bytes 1048608 | tf_op jit(solution)/shard_map/all_to_all | solution.py:46
  209.2 4.2 %all-to-all-start.4 = ((bf16[8,32,2,1024]{3,1,2,0:T(8,128)(2,1)}), bf16[8,32,2,1024]{3,1,2,0:T(8,128)(2,1)}, u32[]{:S(2)}, u32[]{:S(2)}) async-start(bf16[8,32,2,1024]{3,1,2,0:T(8,128)(2,1)} %get-tuple-element.16), calls=%async_computation.4 | async-start | bytes 2097152 | tf_op jit(solution)/shard_map/all_to_all | solution.py:46
  213.4 6.6 %fusion.1 = f32[1,1024,1024]{2,1,0:T(8,128)} fusion(f32[1,1024,1024]{2,1,0:T(8,128)} %param.11, bf16[64,16,1024]{2,0,1:T(8,128)(2,1)S(1)} %copy-done.3, f32[]{:T(128)S(6)} %div.10), kind=kOutput, calls=%fused_computation.6 | convolution fusion | flops 2150629376 | bytes 10485764 | tf_op jit(solution)/shard_map/dot_general | solution.py:77
  220.1 8.8 %all-to-all-done.4 = bf16[8,32,2,1024]{3,1,2,0:T(8,128)(2,1)} async-done(((bf16[8,32,2,1024]{3,1,2,0:T(8,128)(2,1)}), bf16[8,32,2,1024]{3,1,2,0:T(8,128)(2,1)}, u32[]{:S(2)}, u32[]{:S(2)}) %all-to-all-start.4) | async-done | bytes 1048608 | tf_op jit(solution)/shard_map/all_to_all | solution.py:46
  228.9 1.5 pad_maximum_fusion
  230.4 2.0 gather_fusion.3
  232.4 2.0 select_bitcast_fusion
  234.4 1.5 copy.27
  235.9 0.0 copy-done.1
  (20 shorter events, 0.1 us)
Async XLA Ops:
  0.6 125.4 %copy-start = (bf16[1,1024,1024]{2,1,0:T(8,128)(2,1)S(1)}, bf16[1,1024,1024]{2,1,0:T(8,128)(2,1)}, u32[]{:S(2)}) copy-start(bf16[1,1024,1024]{2,1,0:T(8,128)(2,1)} %param.13) | copy-start | bytes 6291460
  12.7 39.1 %all-to-all-start = ((bf16[64,16,1024]{2,0,1:T(8,128)(2,1)}), bf16[64,16,1024]{2,0,1:T(8,128)(2,1)}, u32[]{:S(2)}, u32[]{:S(2)}) async-start(bf16[64,16,1024]{2,0,1:T(8,128)(2,1)} %select_bitcast_fusion.2), calls=%async_computation | async-start | bytes 4194304 | tf_op jit(solution)/shard_map/all_to_all | solution.py:63
  89.7 1.3 copy-start.2
  141.4 31.8 %all-to-all-start.2 = ((bf16[16,2,32768]{2,1,0:T(2,128)(2,1)}), bf16[16,2,32768]{2,1,0:T(2,128)(2,1)S(1)}, u32[]{:S(2)}, u32[]{:S(2)}) async-start(bf16[16,2,32768]{2,1,0:T(2,128)(2,1)} %reshape.98), calls=%async_computation.2 | async-start | bytes 4194304 | tf_op jit(solution)/shard_map/all_to_all | solution.py:87
  188.3 5.1 %copy-start.3 = (bf16[64,16,1024]{2,0,1:T(8,128)(2,1)S(1)}, bf16[64,16,1024]{2,0,1:T(8,128)(2,1)}, u32[]{:S(2)}) copy-start(bf16[64,16,1024]{2,0,1:T(8,128)(2,1)} %copy-done.2) | copy-start | bytes 6291460
  188.3 20.9 %all-to-all-start.3 = ((bf16[8,32,2,1024]{3,1,2,0:T(8,128)(2,1)}), bf16[8,32,2,1024]{3,1,2,0:T(8,128)(2,1)S(1)}, u32[]{:S(2)}, u32[]{:S(2)}) async-start(bf16[8,32,2,1024]{3,1,2,0:T(8,128)(2,1)} %get-tuple-element.15), calls=%async_computation.3 | async-start | bytes 2097152 | tf_op jit(solution)/shard_map/all_to_all | solution.py:46
  209.2 19.7 %all-to-all-start.4 = ((bf16[8,32,2,1024]{3,1,2,0:T(8,128)(2,1)}), bf16[8,32,2,1024]{3,1,2,0:T(8,128)(2,1)}, u32[]{:S(2)}, u32[]{:S(2)}) async-start(bf16[8,32,2,1024]{3,1,2,0:T(8,128)(2,1)} %get-tuple-element.16), calls=%async_computation.4 | async-start | bytes 2097152 | tf_op jit(solution)/shard_map/all_to_all | solution.py:46
  232.4 3.5 %copy-start.1 = (bf16[1,1024,1024]{2,1,0:T(8,128)(2,1)S(1)}, bf16[1,1024,1024]{2,1,0:T(8,128)(2,1)}, u32[]{:S(2)}) copy-start(bf16[1,1024,1024]{2,1,0:T(8,128)(2,1)} %param.13) | copy-start | bytes 6291460
where the time goes:
time: 238 us; the launch traced here: 236 us
  waiting for transfers between devices  73.8 us (31%)
  blocking collectives  65 us (27%)
  local copies, waits for them, and re-layouts  32.9 us (14%)
  matrix products  21.3 us (9%)
  starting transfers between devices  20.8 us (9%)
  other arithmetic  20.4 us (9%)
    psum x5, blocking collectives, by_axis(): return functools.reduce(lax.psum, axes, shard)  32.6 us
    all_to_all x1, blocking collectives, per_device(): lax.all_to_all(sectioned, MP, split_axis=1, concat_axis=0, tiled=True)  32.4 us
    all_to_all x1, waiting for transfers between devices, per_device(): lax.all_to_all(update_block.reshape(BLK, 1, BLK), MP, split_axis=0, conca...  28 us
    all_to_all x1, waiting for transfers between devices, per_device(): lax.all_to_all(outbound, DP, split_axis=1, concat_axis=1, tiled=True)  27.8 us
    all_to_all x2, waiting for transfers between devices, cut_exchange(): lax.all_to_all(slab, axis, split_axis=0, concat_axis=0, tiled=True)  18.1 us
    unnamed x11, local copies, waits for them, and re-layouts  13.8 us
    all_to_all x2, starting transfers between devices, cut_exchange(): lax.all_to_all(slab, axis, split_axis=0, concat_axis=0, tiled=True)  9.26 us
    dot_general x1, matrix products, per_device(): jnp.dot(partial_left, right_root[0], preferred_element_type=jnp.float32)  8.13 us
  transfers between devices with their start and end apart: 4, of which 4 were waited for; matrix products, arithmetic and copies ran while one was open for 7% of the time, Pallas kernels for 0%

commit v1 on v0

v1 whole, which is shorter than its diff:
```python
import functools

import jax
import jax.numpy as jnp
from jax import lax
from jax.experimental import pallas as pl
from jax.experimental.pallas import tpu as pltpu
from jax.sharding import PartitionSpec as P

MESH = pl.DeviceIdType.MESH
BLK = 1024
DPN = 8
MPN = 16
SHARD = 64
ROWT = 16
KR = SHARD // ROWT
KC = 2
K = KR * KC
WID = BLK // KC
AHEAD = 3
BEHIND = 2
TILE = 256

clip_level = 0.5
beta_stat = 0.95


def xor(value, mask):
    bit = 1
    while bit <= mask:
        if mask & bit:
            value = value + bit * (1 - 2 * ((value // bit) % 2))
        bit *= 2
    return value


def kernel(
    tab, grad, left, right, lroot, rroot, new_left, new_right, update, *scratch
):
    it = iter(scratch)
    gb = [next(it) for _ in range(KR)]
    s1 = next(it)
    r1 = [next(it) for _ in range(K)]
    s2 = next(it)
    gq = next(it)
    s3 = next(it)
    r3 = [next(it) for _ in range(K)]
    s4 = next(it)
    r5 = [next(it) for _ in range(K)]
    ob = next(it)
    lb, rb, la, pb = next(it), next(it), next(it), next(it)
    lst, rst = next(it), next(it)
    sq_own, sq_in1, sq_mid, sq_in2 = next(it), next(it), next(it), next(it)
    ssem, rsem, qs, qr, gsem, wsem, osem, tsem = (next(it) for _ in range(8))

    dp = lax.axis_index("dp")
    mp = lax.axis_index("mp")
    dp_peer = [(xor(dp, i), xor(mp, 8 * (i % 2))) for i in range(DPN)]
    mp_peer = [(dp, xor(mp, q)) for q in range(MPN)]

    barrier = pltpu.get_barrier_semaphore()
    for peer in dp_peer[1:] + mp_peer[1:]:
        pl.semaphore_signal(barrier, inc=1, device_id=peer, device_id_type=MESH)

    for r in range(KR):
        for n in range(MPN):
            here = (pl.ds(ROWT * r, ROWT), pl.ds(BLK * n, BLK))
            pltpu.make_async_copy(grad.at[here], gb[r].at[n], gsem.at[r]).start()

    def send(src, dst, phase, k, peer):
        pltpu.make_async_remote_copy(
            src_ref=src,
            dst_ref=dst,
            send_sem=ssem.at[phase, k],
            recv_sem=rsem.at[phase, k],
            device_id=peer,
            device_id_type=MESH,
        ).start()

    def take_bytes(ref, sem):
        pltpu.make_async_copy(ref, ref, sem).wait()

    seen = set()

    def first_hop(k):
        r, c = k // KC, k % KC
        if r not in seen:
            seen.add(r)
            take_bytes(gb[r], gsem.at[r])
        for i in list(range(1, DPN)) + [0]:
            for n in (2 * i, 2 * i + 1):
                piece = gb[r][tab[n], :, pl.ds(c * WID, WID)]
                if i:
                    s1[k, n] = piece
                else:
                    r1[k][n] = piece
            if i:
                if k == 0 and i == 1:
                    pl.semaphore_wait(barrier, DPN - 1 + MPN - 1)
                pair = pl.ds(2 * i, 2)
                send(s1.at[k, pair], r1[k].at[pair], 0, k, dp_peer[i])

    half, low = mp // 8, mp % 8

    def second_hop(k):
        r, c = k // KC, k % KC
        take_bytes(s1.at[k, pl.ds(2, MPN - 2)], rsem.at[0, k])
        for q in list(range(1, MPN)) + [0]:
            piece = r1[k][tab[16 + q]]
            here = gq.at[half, low, r, :, pl.ds(c * WID, WID)]
            if q:
                s2[k, q] = piece
                send(s2.at[k, q], here, 1, k, mp_peer[q])
            else:
                gq[half, low, r, :, pl.ds(c * WID, WID)] = piece

    def square_tile(r, acc):
        def body(n, acc):
            x = gb[r][n].astype(jnp.float32)
            x = x * x
            for w in range(BLK // 128):
                acc = acc + x[:8, w * 128 : (w + 1) * 128] + x[8:, w * 128 : (w + 1) * 128]
            return acc

        return lax.fori_loop(0, MPN, body, acc)

    def send_square(src, dst, stage, peer):
        pltpu.make_async_remote_copy(
            src_ref=src,
            dst_ref=dst,
            send_sem=qs.at[stage],
            recv_sem=qr.at[stage],
            device_id=peer,
            device_id_type=MESH,
        ).start()

    for k in range(min(AHEAD, K)):
        first_hop(k)
    for r in range(KR):
        if r not in seen:
            seen.add(r)
            take_bytes(gb[r], gsem.at[r])
    loads = [
        pltpu.make_async_copy(lroot, lb, wsem.at[0]),
        pltpu.make_async_copy(rroot, rb, wsem.at[1]),
        pltpu.make_async_copy(left, lst, wsem.at[2]),
        pltpu.make_async_copy(right, rst, wsem.at[3]),
    ]
    for c in loads:
        c.start()
    acc = jnp.zeros((8, 128), jnp.float32)
    for r in range(KR):
        acc = square_tile(r, acc)
    sq_own[...] = acc
    for i in range(1, DPN):
        send_square(sq_own, sq_in1.at[i], 0, dp_peer[i])
    for k in range(K):
        second_hop(k)
        if k + AHEAD < K:
            first_hop(k + AHEAD)
        if k == 1:
            take_bytes(sq_in1.at[pl.ds(1, DPN - 1)], qr.at[0])
            mid = sq_own[...]
            for i in range(1, DPN):
                mid = mid + sq_in1[i]
            sq_mid[...] = mid
            for q in range(1, MPN):
                send_square(sq_mid, sq_in2.at[q], 1, mp_peer[q])
    for c in loads:
        c.wait()
    take_bytes(sq_in2.at[pl.ds(1, MPN - 1)], qr.at[1])
    total = sq_mid[...]
    for q in range(1, MPN):
        total = total + sq_in2[q]
    total = jnp.sum(jnp.sum(total, axis=0, keepdims=True), axis=1, keepdims=True)
    mean_square = total / (DPN * BLK * MPN * BLK)
    scale = clip_level / jnp.sqrt(mean_square + 1e-06)
    factor = (1.0 - beta_stat) * scale * scale / BLK
    for k in range(K):
        take_bytes(s2.at[k, pl.ds(1, MPN - 1)], rsem.at[1, k])

    side = [tab[64], tab[65]]
    rows = MPN * ROWT

    def third_hop(k):
        r, c = k // KC, k % KC
        if c == 0:
            for h in range(2):
                la[pl.ds(h * rows // 2, rows // 2), :] = lb[side[h], :, r].reshape(
                    rows // 2, BLK
                )

            @pl.loop(0, BLK // TILE)
            def _(n):
                at = pl.ds(pl.multiple_of(n * TILE, TILE), TILE)
                out = jnp.dot(
                    la[:, : BLK // 2],
                    gq[side[0], :, :, :, at].reshape(BLK // 2, TILE),
                    preferred_element_type=jnp.float32,
                )
                out += jnp.dot(
                    la[:, BLK // 2 :],
                    gq[side[1], :, :, :, at].reshape(BLK // 2, TILE),
                    preferred_element_type=jnp.float32,
                )
                pb[:, at] = out.astype(jnp.bfloat16)

        for n in range(WID // TILE):
            out = jnp.dot(
                pb[...],
                rb[:, pl.ds(c * WID + n * TILE, TILE)],
                preferred_element_type=jnp.float32,
            )
            out = (out * scale).astype(jnp.bfloat16)
            s3[k, :, :, pl.ds(n * TILE, TILE)] = out.reshape(MPN, ROWT, TILE)
        for q in range(1, MPN):
            send(s3.at[k, mp_peer[q][1]], r3[k].at[q], 2, k, mp_peer[q])
        r3[k][0] = s3[k, mp]

    def fourth_hop(k):
        take_bytes(s2.at[k, pl.ds(1, MPN - 1)], rsem.at[2, k])
        for i in list(range(1, DPN)) + [0]:
            for n in (2 * i, 2 * i + 1):
                piece = r3[k][tab[32 + n]]
                if i:
                    s4[k, n] = piece
                else:
                    r5[k][n] = piece
            if i:
                pair = pl.ds(2 * i, 2)
                send(s4.at[k, pair], r5[k].at[pair], 3, k, dp_peer[i])

    stats_out = []

    def left_part(n):
        here = pl.ds(n * TILE, TILE)
        tiles = TILE // SHARD
        lhs = gq[side[n // 2], pl.ds((n % 2) * tiles, tiles)].reshape(TILE, BLK)
        for g in range(2):
            cols = pl.ds(g * BLK // 2, BLK // 2)
            gram = lax.dot_general(
                lhs,
                gq[side[g]].reshape(BLK // 2, BLK),
                (((1,), (1,)), ((), ())),
                preferred_element_type=jnp.float32,
            )
            lst[here, cols] = beta_stat * lst[here, cols] + factor * gram
        c = pltpu.make_async_copy(lst.at[here], new_left.at[here], tsem.at[n])
        c.start()
        stats_out.append(c)

    def right_part(n):
        here = pl.ds(n * TILE, TILE)
        gram = lax.dot_general(
            gq[:, :, :, :, here].reshape(BLK, TILE),
            gq[...].reshape(BLK, BLK),
            (((0,), (0,)), ((), ())),
            preferred_element_type=jnp.float32,
        )
        rst[here, :] = beta_stat * rst[here, :] + factor * gram
        c = pltpu.make_async_copy(rst.at[here], new_right.at[here], tsem.at[4 + n])
        c.start()
        stats_out.append(c)

    parts = [functools.partial(left_part, n) for n in range(4)]
    parts += [functools.partial(right_part, n) for n in range(4)]

    for k in range(K + BEHIND):
        if k < K:
            third_hop(k)
        if k >= BEHIND:
            fourth_hop(k - BEHIND)
            if parts:
                parts.pop(0)()
    for part in parts:
        part()

    update_out = []
    for k in range(K):
        r, c = k // KC, k % KC
        take_bytes(s1.at[k, pl.ds(2, MPN - 2)], rsem.at[3, k])
        for col in range(MPN):
            here = pl.ds(col * BLK + c * WID, WID)
            ob[pl.ds(r * ROWT, ROWT), here] = r5[k][tab[48 + col]]
        if c == KC - 1:
            here = pl.ds(r * ROWT, ROWT)
            cp = pltpu.make_async_copy(ob.at[here], update.at[here], osem.at[r])
            cp.start()
            update_out.append(cp)

    for k in range(K):
        take_bytes(s1.at[k, pl.ds(2, MPN - 2)], ssem.at[0, k])
        take_bytes(s2.at[k, pl.ds(1, MPN - 1)], ssem.at[1, k])
        take_bytes(s2.at[k, pl.ds(1, MPN - 1)], ssem.at[2, k])
        take_bytes(s1.at[k, pl.ds(2, MPN - 2)], ssem.at[3, k])
    take_bytes(sq_in1.at[pl.ds(1, DPN - 1)], qs.at[0])
    take_bytes(sq_in2.at[pl.ds(1, MPN - 1)], qs.at[1])
    for cp in stats_out + update_out:
        cp.wait()


def tables(block_owner, dp, mp):
    owner = block_owner.reshape(DPN, MPN)
    rank = jnp.sum((owner[:, None, :] < owner[:, :, None]).astype(jnp.int32), axis=2)
    sixteen = jnp.arange(MPN, dtype=jnp.int32)
    mine = lax.dynamic_index_in_dim(rank, dp, 0, keepdims=False)
    col_slot = ((mine // 2) ^ dp) * 2 + mine % 2
    slot_col = jnp.sum(
        jnp.where(col_slot[None, :] == sixteen[:, None], sixteen[None, :], 0), axis=1
    )
    bands = jnp.arange(DPN, dtype=jnp.int32)
    slot = ((bands ^ dp) * 2)[:, None] + rank % 2
    want = dp * MPN + (mp ^ sixteen)
    hop_slot = jnp.sum(
        jnp.where(owner[None] == want[:, None, None], slot[None], 0), axis=(1, 2)
    )
    slot_hop = jnp.sum(
        jnp.where(hop_slot[None, :] == sixteen[:, None], sixteen[None, :], 0), axis=1
    )
    flipped = (hop_slot[:1] // 2) % 2
    return jnp.concatenate(
        [slot_col, hop_slot, slot_hop, col_slot, flipped, 1 - flipped]
    )


def per_device(grad, block_owner, left_stat, right_stat, left_root, right_root):
    dp = lax.axis_index("dp")
    mp = lax.axis_index("mp")
    tab = tables(block_owner, dp, mp)
    bf, f32 = jnp.bfloat16, jnp.float32
    hbm = pl.BlockSpec(memory_space=pl.ANY)
    hop = (MPN, ROWT, WID)
    dma = pltpu.SemaphoreType.DMA
    new_left, new_right, update = pl.pallas_call(
        kernel,
        name="shampoo",
        out_shape=(
            jax.ShapeDtypeStruct((BLK, BLK), f32),
            jax.ShapeDtypeStruct((BLK, BLK), f32),
            jax.ShapeDtypeStruct(grad.shape, bf),
        ),
        in_specs=[pl.BlockSpec(memory_space=pltpu.SMEM)]
        + [pl.BlockSpec(memory_space=pltpu.HBM)] * 5,
        out_specs=(hbm, hbm, hbm),
        scratch_shapes=[pltpu.VMEM((MPN, ROWT, BLK), bf) for _ in range(KR)]
        + [pltpu.VMEM((K, *hop), bf)]
        + [pltpu.VMEM(hop, bf) for _ in range(K)]
        + [pltpu.VMEM((K, *hop), bf)]
        + [pltpu.VMEM((2, 8, KR, ROWT, BLK), bf)]
        + [pltpu.VMEM((K, *hop), bf)]
        + [pltpu.VMEM(hop, bf) for _ in range(K)]
        + [pltpu.VMEM((K, *hop), bf)]
        + [pltpu.VMEM(hop, bf) for _ in range(K)]
        + [pltpu.VMEM((SHARD, MPN * BLK), bf)]
        + [
            pltpu.VMEM((2, 8, KR, ROWT, BLK), bf),
            pltpu.VMEM((BLK, BLK), bf),
            pltpu.VMEM((MPN * ROWT, BLK), bf),
            pltpu.VMEM((MPN * ROWT, BLK), bf),
            pltpu.VMEM((BLK, BLK), f32),
            pltpu.VMEM((BLK, BLK), f32),
            pltpu.VMEM((8, 128), f32),
            pltpu.VMEM((DPN, 8, 128), f32),
            pltpu.VMEM((8, 128), f32),
            pltpu.VMEM((MPN, 8, 128), f32),
            dma((4, K)),
            dma((4, K)),
            dma((2,)),
            dma((2,)),
            dma((KR,)),
            dma((4,)),
            dma((KR,)),
            dma((8,)),
        ],
        compiler_params=pltpu.CompilerParams(
            collective_id=0, has_side_effects=True, vmem_limit_bytes=48 << 20
        ),
    )(
        tab,
        grad,
        left_stat[0],
        right_stat[0],
        left_root[0].reshape(2, 8, KR, ROWT, BLK),
        right_root[0],
    )
    return (new_left[None], new_right[None], update)


def solution(mesh):
    both = ("dp", "mp")
    in_specs = (
        P(both, None),
        P(),
        P(both, None, None),
        P(both, None, None),
        P(both, None, None),
        P(both, None, None),
    )
    out_specs = (P(both, None, None), P(both, None, None), P(both, None))
    return jax.shard_map(
        per_device, mesh=mesh, in_specs=in_specs, out_specs=out_specs, check_vma=False
    )
```

time: 238 us -> 89.9 us (0.38)
  Pallas kernels: 0 us -> 76.3 us
  waiting for transfers between devices: 73.8 us -> 0 us
  blocking collectives: 65 us -> 0 us
  local copies, waits for them, and re-layouts: 32.9 us -> 10.7 us
  matrix products: 21.3 us -> 0 us
  starting transfers between devices: 20.8 us -> 0 us
  other arithmetic: 20.4 us -> 0.97 us
    pallas_call x0 -> x1, Pallas kernels: none -> 76.3 us  [per_device(): pl.pallas_call(kernel, name='shampoo', out_shape=(jax.ShapeDtypeStruct((B...]
    all_to_all x4 -> x0, waiting for transfers between devices: 73.8 us -> none  [the longest x1 28 us: per_device(): lax.all_to_all(update_block.reshape(BLK, 1, BLK), MP, split_axis=0, conca...]
    psum x5 -> x0, blocking collectives: 32.6 us -> none  [by_axis(): return functools.reduce(lax.psum, axes, shard)]
    all_to_all x1 -> x0, blocking collectives: 32.4 us -> none  [per_device(): lax.all_to_all(sectioned, MP, split_axis=1, concat_axis=0, tiled=True)]
    dot_general x3 -> x0, matrix products: 21.3 us -> none  [the longest x1 8.13 us: per_device(): jnp.dot(partial_left, right_root[0], preferred_element_type=jnp.float32)]
    all_to_all x4 -> x0, starting transfers between devices: 20.8 us -> none  [the longest x2 9.26 us: cut_exchange(): lax.all_to_all(slab, axis, split_axis=0, concat_axis=0, tiled=True)]
    gather x4 -> x0, local copies, waits for them, and re-layouts: 11.2 us -> none  [the longest x1 3.59 us: per_device(): sectioned = jnp.take(banded, jnp.argsort(owner_cols), axis=1)]
    select_n x7 -> x0, other arithmetic: 6.89 us -> none  [the longest x2 3.18 us: per_device(): outbound = jnp.take(pieces, column_order, axis=1)]
  transfers between devices with their start and end apart: 4 -> 0, of which waited for: 4 -> 0; matrix products, arithmetic and copies ran while one was open for 7% -> 0% of each run, Pallas kernels for 0% -> 0%
where the time goes in v1:
time: 89.9 us; the launch traced here: 88.9 us
  Pallas kernels  76.3 us (85%)
  local copies, waits for them, and re-layouts  10.7 us (12%)
  other arithmetic  0.97 us (1%)
    pallas_call x1, Pallas kernels, per_device(): pl.pallas_call(kernel, name='shampoo', out_shape=(jax.ShapeDtypeStruct((B...  76.3 us
    unnamed x7, local copies, waits for them, and re-layouts  9.87 us

profile of v1, /device:TPU:0, one launch (start us, length us, event | category | flops | bytes accessed | tf_op | source)
XLA Modules:
  0.0 88.9 jit_solution(3513037316554599135)
XLA Ops:
  0.7 0.7 lt.39
  1.4 0.3 convert_reduce_fusion
  1.7 0.1 fusion.1
  1.8 0.4 select_reduce_fusion
  2.4 0.1 select_reduce_fusion.1
  2.6 0.1 concatenate.3.tab
  2.6 0.0 copy-start
  2.6 1.6 %copy-done = bf16[64,16384]{1,0:T(8,128)(2,1)S(1)} copy-done((bf16[64,16384]{1,0:T(8,128)(2,1)S(1)}, bf16[64,16384]{1,0:T(8,128)(2,1)}, u32[]{:S(2)}) %copy-start) | copy-done | bytes 2097176
  4.2 76.3 %shampoo.1 = (f32[1024,1024]{1,0:T(8,128)}, f32[1024,1024]{1,0:T(8,128)}, bf16[64,16384]{1,0:T(8,128)(2,1)S(1)}) custom-call(s32[66]{0:T(128)S(1)} %concatenate.3.tab, bf16[64,16384]{1,0:T(8,128)(2,1)S(1)} %copy-done, f32[1024,1024]{1,0:T(8,128)} %bitcast.22, f32[1024,1024]{1,0:T(8,128)} %bitcast.23, bf16[2,8,4,16,1024]{4,3,2,1,0:T(8,128)(2,1)} %bitcast.26, ...), custom_call_target="tpu_custom_call" | custom-call | tf_op jit(solution)/shard_map/shampoo/pallas_call | solution.py:334
  80.6 0.0 copy-start.1
  80.6 4.9 %copy.12 = f32[1,1024,1024]{2,1,0:T(8,128)} copy(f32[1,1024,1024]{2,1,0:T(8,128)} %bitcast.25) | data formatting | bytes 8388608
  85.5 0.0 copy-done.1
  85.5 2.0 %copy.13 = f32[1,1024,1024]{2,1,0:T(8,128)} copy(f32[1,1024,1024]{2,1,0:T(8,128)S(1)} %bitcast.24) | data formatting | bytes 8388608
  87.5 1.3 %copy.14 = bf16[64,16384]{1,0:T(8,128)(2,1)} copy(bf16[64,16384]{1,0:T(8,128)(2,1)S(1)} %get-tuple-element.16) | data formatting | bytes 4194304
  (4 shorter events, 0.1 us)
Async XLA Ops:
  2.6 1.6 %copy-start = (bf16[64,16384]{1,0:T(8,128)(2,1)S(1)}, bf16[64,16384]{1,0:T(8,128)(2,1)}, u32[]{:S(2)}) copy-start(bf16[64,16384]{1,0:T(8,128)(2,1)} %grad.1) | copy-start | bytes 6291460
  80.6 5.0 %copy-start.1 = (f32[1024,1024]{1,0:T(8,128)S(1)}, f32[1024,1024]{1,0:T(8,128)}, u32[]{:S(2)}) copy-start(f32[1024,1024]{1,0:T(8,128)} %get-tuple-element.7) | copy-start | bytes 12582916

commit v2 on v1

--- a/solution.py
+++ b/solution.py
@@ -35,7 +35,7 @@
 
 
 def kernel(
-    tab, grad, left, right, lroot, rroot, new_left, new_right, update, *scratch
+    tab, grad, left, right, lroot, rroot, lst, rst, ob, *scratch
 ):
     it = iter(scratch)
     gb = [next(it) for _ in range(KR)]
@@ -47,11 +47,9 @@
     r3 = [next(it) for _ in range(K)]
     s4 = next(it)
     r5 = [next(it) for _ in range(K)]
-    ob = next(it)
     lb, rb, la, pb = next(it), next(it), next(it), next(it)
-    lst, rst = next(it), next(it)
     sq_own, sq_in1, sq_mid, sq_in2 = next(it), next(it), next(it), next(it)
-    ssem, rsem, qs, qr, gsem, wsem, osem, tsem = (next(it) for _ in range(8))
+    ssem, rsem, qs, qr, gsem, wsem = (next(it) for _ in range(6))
 
     dp = lax.axis_index("dp")
     mp = lax.axis_index("mp")
@@ -230,8 +228,6 @@
                 pair = pl.ds(2 * i, 2)
                 send(s4.at[k, pair], r5[k].at[pair], 3, k, dp_peer[i])
 
-    stats_out = []
-
     def left_part(n):
         here = pl.ds(n * TILE, TILE)
         tiles = TILE // SHARD
@@ -245,9 +241,6 @@
                 preferred_element_type=jnp.float32,
             )
             lst[here, cols] = beta_stat * lst[here, cols] + factor * gram
-        c = pltpu.make_async_copy(lst.at[here], new_left.at[here], tsem.at[n])
-        c.start()
-        stats_out.append(c)
 
     def right_part(n):
         here = pl.ds(n * TILE, TILE)
@@ -258,9 +251,6 @@
             preferred_element_type=jnp.float32,
         )
         rst[here, :] = beta_stat * rst[here, :] + factor * gram
-        c = pltpu.make_async_copy(rst.at[here], new_right.at[here], tsem.at[4 + n])
-        c.start()
-        stats_out.append(c)
 
     parts = [functools.partial(left_part, n) for n in range(4)]
     parts += [functools.partial(right_part, n) for n in range(4)]
@@ -275,18 +265,12 @@
     for part in parts:
         part()
 
-    update_out = []
     for k in range(K):
         r, c = k // KC, k % KC
         take_bytes(s1.at[k, pl.ds(2, MPN - 2)], rsem.at[3, k])
         for col in range(MPN):
             here = pl.ds(col * BLK + c * WID, WID)
             ob[pl.ds(r * ROWT, ROWT), here] = r5[k][tab[48 + col]]
-        if c == KC - 1:
-            here = pl.ds(r * ROWT, ROWT)
-            cp = pltpu.make_async_copy(ob.at[here], update.at[here], osem.at[r])
-            cp.start()
-            update_out.append(cp)
 
     for k in range(K):
         take_bytes(s1.at[k, pl.ds(2, MPN - 2)], ssem.at[0, k])
@@ -295,29 +279,40 @@
         take_bytes(s1.at[k, pl.ds(2, MPN - 2)], ssem.at[3, k])
     take_bytes(sq_in1.at[pl.ds(1, DPN - 1)], qs.at[0])
     take_bytes(sq_in2.at[pl.ds(1, MPN - 1)], qs.at[1])
-    for cp in stats_out + update_out:
-        cp.wait()
-
-
-def tables(block_owner, dp, mp):
-    owner = block_owner.reshape(DPN, MPN)
-    rank = jnp.sum((owner[:, None, :] < owner[:, :, None]).astype(jnp.int32), axis=2)
+
+
+def move(*refs):
+    count = (len(refs) - 1) // 2
+    copies = [
+        pltpu.make_async_copy(refs[n], refs[count + n], refs[-1].at[n])
+        for n in range(count)
+    ]
+    for c in copies:
+        c.start()
+    for c in copies:
+        c.wait()
+
+
+def tables(owner, dp, mp):
+    block = jnp.arange(DPN * MPN, dtype=jnp.int32)
     sixteen = jnp.arange(MPN, dtype=jnp.int32)
-    mine = lax.dynamic_index_in_dim(rank, dp, 0, keepdims=False)
-    col_slot = ((mine // 2) ^ dp) * 2 + mine % 2
+    band = block // MPN
+    before = (band[:, None] == band[None, :]) & (owner[None, :] < owner[:, None])
+    rank = jnp.sum(before.astype(jnp.int32), axis=1)
+    mine = lax.dynamic_slice_in_dim(rank, dp * MPN, MPN)
+    col_slot = ((mine >> 1) ^ dp) * 2 + (mine & 1)
     slot_col = jnp.sum(
         jnp.where(col_slot[None, :] == sixteen[:, None], sixteen[None, :], 0), axis=1
     )
-    bands = jnp.arange(DPN, dtype=jnp.int32)
-    slot = ((bands ^ dp) * 2)[:, None] + rank % 2
+    slot = (band ^ dp) * 2 + (rank & 1)
     want = dp * MPN + (mp ^ sixteen)
     hop_slot = jnp.sum(
-        jnp.where(owner[None] == want[:, None, None], slot[None], 0), axis=(1, 2)
+        jnp.where(owner[None, :] == want[:, None], slot[None, :], 0), axis=1
     )
     slot_hop = jnp.sum(
         jnp.where(hop_slot[None, :] == sixteen[:, None], sixteen[None, :], 0), axis=1
     )
-    flipped = (hop_slot[:1] // 2) % 2
+    flipped = (hop_slot[:1] >> 1) & 1
     return jnp.concatenate(
         [slot_col, hop_slot, slot_hop, col_slot, flipped, 1 - flipped]
     )
@@ -331,17 +326,15 @@
     hbm = pl.BlockSpec(memory_space=pl.ANY)
     hop = (MPN, ROWT, WID)
     dma = pltpu.SemaphoreType.DMA
-    new_left, new_right, update = pl.pallas_call(
+    vmem = pl.BlockSpec(memory_space=pltpu.VMEM)
+    outs = (((BLK, BLK), f32), ((BLK, BLK), f32), (grad.shape, bf))
+    done = pl.pallas_call(
         kernel,
         name="shampoo",
-        out_shape=(
-            jax.ShapeDtypeStruct((BLK, BLK), f32),
-            jax.ShapeDtypeStruct((BLK, BLK), f32),
-            jax.ShapeDtypeStruct(grad.shape, bf),
-        ),
+        out_shape=tuple(pltpu.VMEM(*o) for o in outs),
         in_specs=[pl.BlockSpec(memory_space=pltpu.SMEM)]
         + [pl.BlockSpec(memory_space=pltpu.HBM)] * 5,
-        out_specs=(hbm, hbm, hbm),
+        out_specs=(vmem, vmem, vmem),
         scratch_shapes=[pltpu.VMEM((MPN, ROWT, BLK), bf) for _ in range(KR)]
         + [pltpu.VMEM((K, *hop), bf)]
         + [pltpu.VMEM(hop, bf) for _ in range(K)]
@@ -351,14 +344,11 @@
         + [pltpu.VMEM(hop, bf) for _ in range(K)]
         + [pltpu.VMEM((K, *hop), bf)]
         + [pltpu.VMEM(hop, bf) for _ in range(K)]
-        + [pltpu.VMEM((SHARD, MPN * BLK), bf)]
         + [
             pltpu.VMEM((2, 8, KR, ROWT, BLK), bf),
             pltpu.VMEM((BLK, BLK), bf),
             pltpu.VMEM((MPN * ROWT, BLK), bf),
             pltpu.VMEM((MPN * ROWT, BLK), bf),
-            pltpu.VMEM((BLK, BLK), f32),
-            pltpu.VMEM((BLK, BLK), f32),
             pltpu.VMEM((8, 128), f32),
             pltpu.VMEM((DPN, 8, 128), f32),
             pltpu.VMEM((8, 128), f32),
@@ -369,11 +359,9 @@
             dma((2,)),
             dma((KR,)),
             dma((4,)),
-            dma((KR,)),
-            dma((8,)),
         ],
         compiler_params=pltpu.CompilerParams(
-            collective_id=0, has_side_effects=True, vmem_limit_bytes=48 << 20
+            collective_id=0, has_side_effects=True, vmem_limit_bytes=44 << 20
         ),
     )(
         tab,
@@ -383,6 +371,15 @@
         left_root[0].reshape(2, 8, KR, ROWT, BLK),
         right_root[0],
     )
+    new_left, new_right, update = pl.pallas_call(
+        move,
+        name="move",
+        out_shape=tuple(jax.ShapeDtypeStruct(*o) for o in outs),
+        in_specs=(vmem,) * 3,
+        out_specs=(hbm,) * 3,
+        scratch_shapes=[dma((3,))],
+        compiler_params=pltpu.CompilerParams(vmem_limit_bytes=1 << 20),
+    )(*(pltpu.with_memory_space_constraint(d, pltpu.VMEM) for d in done))
     return (new_left[None], new_right[None], update)
 
 

time: 89.9 us -> 84.7 us (0.942)
  local copies, waits for them, and re-layouts: 10.7 us -> 0.6 us
  Pallas kernels: 76.3 us -> 80.3 us
  other arithmetic: 0.97 us -> 1.96 us
    unnamed x7 -> x0, local copies, waits for them, and re-layouts: 9.87 us -> none
    pallas_call x1 -> x2, Pallas kernels: 76.3 us -> 80.3 us  [the longest x1 76.3 us: per_device(): pl.pallas_call(kernel, name='shampoo', out_shape=tuple((pltpu.VMEM(*o) fo...]
    reduce_sum x2, other arithmetic: 0.73 us -> 1.75 us  [the longest x1 0.91 us: tables(): rank = jnp.sum(before.astype(jnp.int32), axis=1)]
where the time goes in v2:
time: 84.7 us; the launch traced here: 83.6 us
  Pallas kernels  80.3 us (95%)
  other arithmetic  1.96 us (2%)
    pallas_call x1, Pallas kernels, per_device(): pl.pallas_call(kernel, name='shampoo', out_shape=tuple((pltpu.VMEM(*o) fo...  76.3 us
    pallas_call x1, Pallas kernels, per_device(): pl.pallas_call(move, name='move', out_shape=tuple((jax.ShapeDtypeStruct(*...  3.99 us

profile of v2, /device:TPU:0, one launch (start us, length us, event | category | flops | bytes accessed | tf_op | source)
XLA Modules:
  0.0 83.6 jit_solution(13861957492868557404)
XLA Ops:
  0.7 0.9 %convert_reduce_fusion = s32[128]{0:T(128)S(1)} fusion(s32[128]{0:T(128)} %param.7, s32[128]{0:T(128)S(1)} %and_select_fusion), kind=kLoop, calls=%fused_computation | loop fusion | flops 81792 | bytes 1536 | tf_op jit(solution)/shard_map/reduce_sum | solution.py:301
  1.6 0.1 and_add_fusion.1
  1.7 0.8 %select_reduce_fusion.1 = s32[16]{0:T(128)S(1)} fusion(s32[128]{0:T(128)S(1)} %and_add_fusion, s32[128]{0:T(128)} %param.7, s32[16]{0:T(128)S(1)} %xor_add_fusion), kind=kLoop, calls=%fused_computation.3 | loop fusion | flops 6128 | bytes 1152 | tf_op jit(solution)/shard_map/reduce_sum | solution.py:309
  2.5 0.1 select_reduce_fusion
  2.7 0.6 concatenate.3.tab
  3.3 76.3 %shampoo.1 = (f32[1024,1024]{1,0:T(8,128)S(1)}, f32[1024,1024]{1,0:T(8,128)S(1)}, bf16[64,16384]{1,0:T(8,128)(2,1)S(1)}) custom-call(s32[66]{0:T(128)} %concatenate.3.tab, bf16[64,16384]{1,0:T(8,128)(2,1)} %grad.1, f32[1024,1024]{1,0:T(8,128)} %bitcast.7, f32[1024,1024]{1,0:T(8,128)} %bitcast.8, bf16[2,8,4,16,1024]{4,3,2,1,0:T(8,128)(2,1)} %bitcast.9, ...), custom_call_target="tpu_custom_call" | custom-call | tf_op jit(solution)/shard_map/shampoo/pallas_call | solution.py:331
  79.6 4.0 %move.1 = (f32[1024,1024]{1,0:T(8,128)}, f32[1024,1024]{1,0:T(8,128)}, bf16[64,16384]{1,0:T(8,128)(2,1)}) custom-call(f32[1024,1024]{1,0:T(8,128)S(1)} %get-tuple-element.9.refs_0_, f32[1024,1024]{1,0:T(8,128)S(1)} %get-tuple-element.10.refs_1_, bf16[64,16384]{1,0:T(8,128)(2,1)S(1)} %get-tuple-element.11.refs_2_), custom_call_target="tpu_custom_call" | custom-call | tf_op jit(solution)/shard_map/move/pallas_call | solution.py:374
  (3 shorter events, 0.0 us)

commit v3 on v2

v3 whole, which is shorter than its diff:
```python
import functools

import jax
import jax.numpy as jnp
from jax import lax
from jax.experimental import pallas as pl
from jax.experimental.pallas import tpu as pltpu
from jax.sharding import PartitionSpec as P

MESH = pl.DeviceIdType.MESH
BLK = 1024
DPN = 8
MPN = 16
SHARD = 64
ROWT = 16
KR = SHARD // ROWT
CHUNKS = [(row, col, 512) for row in range(4) for col in (0, 512)]
K = len(CHUNKS)
AHEAD = 3
BEHIND = 2
TILE = 256
MOVES = 4

clip_level = 0.5
beta_stat = 0.95


def steps(value, bits):
    return [
        (1 << bit) * (1 - 2 * lax.rem(lax.div(value, 1 << bit), 2)) for bit in range(bits)
    ]


def xor(value, mask, step):
    for bit, amount in enumerate(step):
        if mask >> bit & 1:
            value = value + amount
    return value


def make_tables(owner, dp, mp):
    shape = (DPN * MPN, DPN * MPN)
    down = lax.broadcasted_iota(jnp.int32, shape, 0)
    along = lax.broadcasted_iota(jnp.int32, shape, 1)

    def pick(mask, value):
        return jnp.sum(jnp.where(mask, value, 0), axis=0, keepdims=True)

    across = jnp.broadcast_to(owner, shape)
    mine = jnp.sum(jnp.where(down == along, across, 0), axis=1, keepdims=True)
    mine = jnp.broadcast_to(mine, shape)
    before = ((down >> 4) == (along >> 4)) & (across < mine)
    rank = jnp.sum(jnp.where(before, 1, 0), axis=1, keepdims=True)
    rank = jnp.broadcast_to(rank, shape)
    column = down - dp * MPN
    in_band = (down >> 4) == dp
    sent = ((rank >> 1) ^ dp) * 2 + (rank & 1)
    met = ((down >> 4) ^ dp) * 2 + (rank & 1)
    slot_col = pick(in_band & (sent == along), column)
    hop_slot = pick(mine == dp * MPN + ((along & 15) ^ mp), met)
    slot_hop = pick(((mine >> 4) == dp) & (met == along), (mine & 15) ^ mp)
    col_slot = pick(in_band & (column == along), sent)
    flipped = (pick(mine == dp * MPN + mp, met) >> 1) & 1
    return slot_col, hop_slot, slot_hop, col_slot, flipped, 1 - flipped


def kernel(owners, grad, left, right, lroot, rroot, lst, rst, ob, *scratch):
    it = iter(scratch)

    def take(count):
        return [next(it) for _ in range(count)]

    gb = take(KR)
    s1, r1, s2, s3, r3, s4, r5 = (take(K) for _ in range(7))
    gq, lb, rb, la, pb = take(5)
    own_row, tab_rows, tab = take(3)
    sq_own, sq_in1, sq_mid, sq_in2 = take(4)
    ssem, rsem, qs, qr, gsem, wsem, tsem = take(7)

    dp = lax.axis_index("dp")
    mp = lax.axis_index("mp")
    dp_step, mp_step = steps(dp, 3), steps(mp, 4)
    dp_peer = [
        (xor(dp, i, dp_step), xor(mp, 8 * (i % 2), mp_step)) for i in range(DPN)
    ]
    mp_peer = [(dp, xor(mp, q, mp_step)) for q in range(MPN)]

    barrier = pltpu.get_barrier_semaphore()
    for peer in dp_peer[1:] + mp_peer[1:]:
        pl.semaphore_signal(barrier, inc=1, device_id=peer, device_id_type=MESH)

    load_owners = pltpu.make_async_copy(owners, own_row, tsem.at[0])
    load_owners.start()

    def load_grad(r):
        for n in range(MPN):
            here = (pl.ds(ROWT * r, ROWT), pl.ds(BLK * n, BLK))
            pltpu.make_async_copy(grad.at[here], gb[r].at[n], gsem.at[r]).start()

    load_grad(0)

    load_owners.wait()
    tab_rows[...] = jnp.zeros_like(tab_rows)
    for n, row in enumerate(make_tables(own_row[...], dp, mp)):
        tab_rows[pl.ds(n, 1), :] = row & 15
    load_tables = pltpu.make_async_copy(tab_rows, tab, tsem.at[1])
    load_tables.start()
    load_tables.wait()

    def send(src, dst, phase, k, peer):
        pltpu.make_async_remote_copy(
            src_ref=src,
            dst_ref=dst,
            send_sem=ssem.at[phase, k],
            recv_sem=rsem.at[phase, k],
            device_id=peer,
            device_id_type=MESH,
        ).start()

    def take_bytes(ref, sem):
        pltpu.make_async_copy(ref, ref, sem).wait()

    seen = set()

    def first_hop(k):
        r, c0, width = CHUNKS[k]
        if r not in seen:
            seen.add(r)
            take_bytes(gb[r], gsem.at[r])
        for i in list(range(1, DPN)) + [0]:
            for n in (2 * i, 2 * i + 1):
                piece = gb[r][tab[0, n], :, pl.ds(c0, width)]
                if i:
                    s1[k][n] = piece
                else:
                    r1[k][n] = piece
            if i:
                if k == 0 and i == 1:
                    pl.semaphore_wait(barrier, DPN - 1 + MPN - 1)
                pair = pl.ds(2 * i, 2)
                send(s1[k].at[pair], r1[k].at[pair], 0, k, dp_peer[i])

    half, low = lax.div(mp, 8), lax.rem(mp, 8)

    def second_hop(k):
        r, c0, width = CHUNKS[k]
        take_bytes(s1[k].at[pl.ds(2, MPN - 2)], rsem.at[0, k])
        for q in range(MPN - 1, -1, -1):
            piece = r1[k][tab[1, q]]
            here = gq.at[half, low, r, :, pl.ds(c0, width)]
            if q:
                s2[k][q] = piece
                send(s2[k].at[q], here, 1, k, mp_peer[q])
            else:
                gq[half, low, r, :, pl.ds(c0, width)] = piece

    def square_tile(r, acc):
        def body(n, acc):
            x = gb[r][n].astype(jnp.float32)
            x = x * x
            for w in range(BLK // 128):
                acc = acc + x[:8, w * 128 : (w + 1) * 128] + x[8:, w * 128 : (w + 1) * 128]
            return acc

        return lax.fori_loop(0, MPN, body, acc)

    def send_square(src, dst, stage, peer):
        pltpu.make_async_remote_copy(
            src_ref=src,
            dst_ref=dst,
            send_sem=qs.at[stage],
            recv_sem=qr.at[stage],
            device_id=peer,
            device_id_type=MESH,
        ).start()

    for k in range(min(AHEAD, K)):
        if k == 1:
            for r in range(1, KR):
                load_grad(r)
        first_hop(k)
    for r in range(KR):
        if r not in seen:
            seen.add(r)
            take_bytes(gb[r], gsem.at[r])
    loads = [
        pltpu.make_async_copy(lroot, lb, wsem.at[0]),
        pltpu.make_async_copy(rroot, rb, wsem.at[1]),
        pltpu.make_async_copy(left, lst, wsem.at[2]),
        pltpu.make_async_copy(right, rst, wsem.at[3]),
    ]
    for c in loads:
        c.start()
    acc = jnp.zeros((8, 128), jnp.float32)
    for r in range(KR):
        acc = square_tile(r, acc)
    sq_own[...] = acc
    for i in range(1, DPN):
        send_square(sq_own, sq_in1.at[i], 0, dp_peer[i])
    for k in range(K):
        second_hop(k)
        if k + AHEAD < K:
            first_hop(k + AHEAD)
        if k == 1:
            take_bytes(sq_in1.at[pl.ds(1, DPN - 1)], qr.at[0])
            mid = sq_own[...]
            for i in range(1, DPN):
                mid = mid + sq_in1[i]
            sq_mid[...] = mid
            for q in range(1, MPN):
                send_square(sq_mid, sq_in2.at[q], 1, mp_peer[q])
    for c in loads:
        c.wait()
    take_bytes(sq_in2.at[pl.ds(1, MPN - 1)], qr.at[1])
    total = sq_mid[...]
    for q in range(1, MPN):
        total = total + sq_in2[q]
    total = jnp.sum(jnp.sum(total, axis=0, keepdims=True), axis=1, keepdims=True)
    mean_square = total / (DPN * BLK * MPN * BLK)
    scale = clip_level / jnp.sqrt(mean_square + 1e-06)
    factor = (1.0 - beta_stat) * scale * scale / BLK
    for k in range(K):
        take_bytes(s2[k].at[pl.ds(1, MPN - 1)], rsem.at[1, k])

    side = [tab[4, 0], tab[5, 0]]
    rows = MPN * ROWT

    def third_hop(k):
        r, c0, width = CHUNKS[k]
        if c0 == 0:
            for h in range(2):
                la[pl.ds(h * rows // 2, rows // 2), :] = lb[side[h], :, r].reshape(
                    rows // 2, BLK
                )

            @pl.loop(0, BLK // TILE)
            def _(n):
                at = pl.ds(pl.multiple_of(n * TILE, TILE), TILE)
                out = jnp.dot(
                    la[:, : BLK // 2],
                    gq[side[0], :, :, :, at].reshape(BLK // 2, TILE),
                    preferred_element_type=jnp.float32,
                )
                out += jnp.dot(
                    la[:, BLK // 2 :],
                    gq[side[1], :, :, :, at].reshape(BLK // 2, TILE),
                    preferred_element_type=jnp.float32,
                )
                pb[:, at] = out.astype(jnp.bfloat16)

        for n in range(width // TILE):
            out = jnp.dot(
                pb[...],
                rb[:, pl.ds(c0 + n * TILE, TILE)],
                preferred_element_type=jnp.float32,
            )
            out = (out * scale).astype(jnp.bfloat16)
            s3[k][:, :, pl.ds(n * TILE, TILE)] = out.reshape(MPN, ROWT, TILE)
        for q in range(MPN - 1, 0, -1):
            send(s3[k].at[mp_peer[q][1]], r3[k].at[q], 2, k, mp_peer[q])
        r3[k][0] = s3[k][mp]

    def fourth_hop(k):
        take_bytes(s2[k].at[pl.ds(1, MPN - 1)], rsem.at[2, k])
        for i in list(range(1, DPN)) + [0]:
            for n in (2 * i, 2 * i + 1):
                piece = r3[k][tab[2, n]]
                if i:
                    s4[k][n] = piece
                else:
                    r5[k][n] = piece
            if i:
                pair = pl.ds(2 * i, 2)
                send(s4[k].at[pair], r5[k].at[pair], 3, k, dp_peer[i])

    def left_part(n):
        here = pl.ds(n * TILE, TILE)
        tiles = TILE // SHARD
        lhs = gq[side[n // 2], pl.ds((n % 2) * tiles, tiles)].reshape(TILE, BLK)
        for g in range(2):
            cols = pl.ds(g * BLK // 2, BLK // 2)
            gram = lax.dot_general(
                lhs,
                gq[side[g]].reshape(BLK // 2, BLK),
                (((1,), (1,)), ((), ())),
                preferred_element_type=jnp.float32,
            )
            lst[here, cols] = beta_stat * lst[here, cols] + factor * gram

    def right_part(n):
        here = pl.ds(n * TILE, TILE)
        gram = lax.dot_general(
            gq[:, :, :, :, here].reshape(BLK, TILE),
            gq[...].reshape(BLK, BLK),
            (((0,), (0,)), ((), ())),
            preferred_element_type=jnp.float32,
        )
        rst[here, :] = beta_stat * rst[here, :] + factor * gram

    parts = [functools.partial(left_part, n) for n in range(4)]
    parts += [functools.partial(right_part, n) for n in range(4)]

    for k in range(K + BEHIND):
        if k < K:
            third_hop(k)
        if k >= BEHIND:
            fourth_hop(k - BEHIND)
            if parts:
                parts.pop(0)()
    for part in parts:
        part()

    for k in range(K):
        r, c0, width = CHUNKS[k]
        take_bytes(s1[k].at[pl.ds(2, MPN - 2)], rsem.at[3, k])
        for col in range(MPN):
            here = pl.ds(col * BLK + c0, width)
            ob[pl.ds(r * ROWT, ROWT), here] = r5[k][tab[3, col]]

    for k in range(K):
        take_bytes(s1[k].at[pl.ds(2, MPN - 2)], ssem.at[0, k])
        take_bytes(s2[k].at[pl.ds(1, MPN - 1)], ssem.at[1, k])
        take_bytes(s2[k].at[pl.ds(1, MPN - 1)], ssem.at[2, k])
        take_bytes(s1[k].at[pl.ds(2, MPN - 2)], ssem.at[3, k])
    take_bytes(sq_in1.at[pl.ds(1, DPN - 1)], qs.at[0])
    take_bytes(sq_in2.at[pl.ds(1, MPN - 1)], qs.at[1])


def move(*refs):
    count = (len(refs) - 1) // 2
    copies = []
    for n in range(count):
        rows = refs[n].shape[0] // MOVES
        for part in range(MOVES):
            here = pl.ds(part * rows, rows)
            sem = refs[-1].at[n, part]
            copies.append(
                pltpu.make_async_copy(refs[n].at[here], refs[count + n].at[here], sem)
            )
    for c in copies:
        c.start()
    for c in copies:
        c.wait()


def per_device(grad, block_owner, left_stat, right_stat, left_root, right_root):
    bf, f32 = jnp.bfloat16, jnp.float32
    hbm = pl.BlockSpec(memory_space=pl.ANY)
    hops = [pltpu.VMEM((MPN, ROWT, width), bf) for _, _, width in CHUNKS]
    dma = pltpu.SemaphoreType.DMA
    vmem = pl.BlockSpec(memory_space=pltpu.VMEM)
    outs = (((BLK, BLK), f32), ((BLK, BLK), f32), (grad.shape, bf))
    done = pl.pallas_call(
        kernel,
        name="shampoo",
        out_shape=tuple(pltpu.VMEM(*o) for o in outs),
        in_specs=[pl.BlockSpec(memory_space=pltpu.HBM)] * 6,
        out_specs=(vmem, vmem, vmem),
        scratch_shapes=[pltpu.VMEM((MPN, ROWT, BLK), bf) for _ in range(KR)]
        + hops * 7
        + [
            pltpu.VMEM((2, 8, KR, ROWT, BLK), bf),
            pltpu.VMEM((2, 8, KR, ROWT, BLK), bf),
            pltpu.VMEM((BLK, BLK), bf),
            pltpu.VMEM((MPN * ROWT, BLK), bf),
            pltpu.VMEM((MPN * ROWT, BLK), bf),
            pltpu.VMEM((1, DPN * MPN), jnp.int32),
            pltpu.VMEM((8, DPN * MPN), jnp.int32),
            pltpu.SMEM((8, DPN * MPN), jnp.int32),
            pltpu.VMEM((8, 128), f32),
            pltpu.VMEM((DPN, 8, 128), f32),
            pltpu.VMEM((8, 128), f32),
            pltpu.VMEM((MPN, 8, 128), f32),
            dma((4, K)),
            dma((4, K)),
            dma((2,)),
            dma((2,)),
            dma((KR,)),
            dma((4,)),
            dma((2,)),
        ],
        compiler_params=pltpu.CompilerParams(
            collective_id=0, has_side_effects=True, vmem_limit_bytes=44 << 20
        ),
    )(
        block_owner.reshape(1, DPN * MPN),
        grad,
        left_stat[0],
        right_stat[0],
        left_root[0].reshape(2, 8, KR, ROWT, BLK),
        right_root[0],
    )
    new_left, new_right, update = pl.pallas_call(
        move,
        name="move",
        out_shape=tuple(jax.ShapeDtypeStruct(*o) for o in outs),
        in_specs=(vmem,) * 3,
        out_specs=(hbm,) * 3,
        scratch_shapes=[dma((3, MOVES))],
        compiler_params=pltpu.CompilerParams(vmem_limit_bytes=1 << 20),
    )(*(pltpu.with_memory_space_constraint(d, pltpu.VMEM) for d in done))
    return (new_left[None], new_right[None], update)


def solution(mesh):
    both = ("dp", "mp")
    in_specs = (
        P(both, None),
        P(),
        P(both, None, None),
        P(both, None, None),
        P(both, None, None),
        P(both, None, None),
    )
    out_specs = (P(both, None, None), P(both, None, None), P(both, None))
    return jax.shard_map(
        per_device, mesh=mesh, in_specs=in_specs, out_specs=out_specs, check_vma=False
    )
```

time: 84.7 us -> 79.5 us (0.939); the launches traced: 83.6 us -> 79.2 us
  other arithmetic: 1.96 us -> 0 us
  Pallas kernels: 80.3 us -> 78.6 us
    reduce_sum x3 -> x0, other arithmetic: 1.86 us -> none  [the longest x1 0.91 us: tables(): rank = jnp.sum(before.astype(jnp.int32), axis=1)]
    pallas_call x1, Pallas kernels: 76.3 us -> 74.6 us  [per_device(): pl.pallas_call(kernel, name='shampoo', out_shape=tuple((pltpu.VMEM(*o) fo...]
where the time goes in v3:
time: 79.5 us; the launch traced here: 79.2 us
  Pallas kernels  78.6 us (99%)
    pallas_call x1, Pallas kernels, per_device(): pl.pallas_call(kernel, name='shampoo', out_shape=tuple((pltpu.VMEM(*o) fo...  74.6 us
    pallas_call x1, Pallas kernels, per_device(): pl.pallas_call(move, name='move', out_shape=tuple((jax.ShapeDtypeStruct(*...  4.02 us

profile of v3, /device:TPU:0, one launch (start us, length us, event | category | flops | bytes accessed | tf_op | source)
XLA Modules:
  0.0 79.2 jit_solution(7554819484400044629)
XLA Ops:
  0.6 74.6 %shampoo.1 = (f32[1024,1024]{1,0:T(8,128)S(1)}, f32[1024,1024]{1,0:T(8,128)S(1)}, bf16[64,16384]{1,0:T(8,128)(2,1)S(1)}) custom-call(s32[1,128]{1,0:T(1,128)} %bitcast.11, bf16[64,16384]{1,0:T(8,128)(2,1)} %grad.1, f32[1024,1024]{1,0:T(8,128)} %bitcast.7, f32[1024,1024]{1,0:T(8,128)} %bitcast.8, bf16[2,8,4,16,1024]{4,3,2,1,0:T(8,128)(2,1)} %bitcast.9, ...), custom_call_target="tpu_custom_call" | custom-call | tf_op jit(solution)/shard_map/shampoo/pallas_call | solution.py:353
  75.2 4.0 %move.1 = (f32[1024,1024]{1,0:T(8,128)}, f32[1024,1024]{1,0:T(8,128)}, bf16[64,16384]{1,0:T(8,128)(2,1)}) custom-call(f32[1024,1024]{1,0:T(8,128)S(1)} %get-tuple-element.9.refs_0_, f32[1024,1024]{1,0:T(8,128)S(1)} %get-tuple-element.10.refs_1_, bf16[64,16384]{1,0:T(8,128)(2,1)S(1)} %get-tuple-element.11.refs_2_), custom_call_target="tpu_custom_call" | custom-call | tf_op jit(solution)/shard_map/move/pallas_call | solution.py:393

commit v4 on v3

--- a/solution.py
+++ b/solution.py
@@ -17,8 +17,14 @@
 CHUNKS = [(row, col, 512) for row in range(4) for col in (0, 512)]
 K = len(CHUNKS)
 AHEAD = 3
-BEHIND = 2
+BEHIND = 3
 TILE = 256
+ORDER1 = (1, 2, 3, 4, 5, 6, 7, 0)
+ORDER2 = tuple(range(15, -1, -1))
+ORDER3 = tuple(range(15, 0, -1))
+ORDER4 = (7, 6, 5, 4, 3, 2, 1, 0)
+SUM_AT = -1
+LOAD_AT = (-1, -1, -1, -1)
 MOVES = 4
 
 clip_level = 0.5
@@ -127,7 +133,7 @@
         if r not in seen:
             seen.add(r)
             take_bytes(gb[r], gsem.at[r])
-        for i in list(range(1, DPN)) + [0]:
+        for i in ORDER1:
             for n in (2 * i, 2 * i + 1):
                 piece = gb[r][tab[0, n], :, pl.ds(c0, width)]
                 if i:
@@ -135,7 +141,7 @@
                 else:
                     r1[k][n] = piece
             if i:
-                if k == 0 and i == 1:
+                if k == 0 and i == ORDER1[0]:
                     pl.semaphore_wait(barrier, DPN - 1 + MPN - 1)
                 pair = pl.ds(2 * i, 2)
                 send(s1[k].at[pair], r1[k].at[pair], 0, k, dp_peer[i])
@@ -145,7 +151,7 @@
     def second_hop(k):
         r, c0, width = CHUNKS[k]
         take_bytes(s1[k].at[pl.ds(2, MPN - 2)], rsem.at[0, k])
-        for q in range(MPN - 1, -1, -1):
+        for q in ORDER2:
             piece = r1[k][tab[1, q]]
             here = gq.at[half, low, r, :, pl.ds(c0, width)]
             if q:
@@ -179,29 +185,36 @@
             for r in range(1, KR):
                 load_grad(r)
         first_hop(k)
-    for r in range(KR):
-        if r not in seen:
-            seen.add(r)
-            take_bytes(gb[r], gsem.at[r])
     loads = [
         pltpu.make_async_copy(lroot, lb, wsem.at[0]),
         pltpu.make_async_copy(rroot, rb, wsem.at[1]),
         pltpu.make_async_copy(left, lst, wsem.at[2]),
         pltpu.make_async_copy(right, rst, wsem.at[3]),
     ]
-    for c in loads:
-        c.start()
-    acc = jnp.zeros((8, 128), jnp.float32)
-    for r in range(KR):
-        acc = square_tile(r, acc)
-    sq_own[...] = acc
-    for i in range(1, DPN):
-        send_square(sq_own, sq_in1.at[i], 0, dp_peer[i])
-    for k in range(K):
-        second_hop(k)
-        if k + AHEAD < K:
-            first_hop(k + AHEAD)
-        if k == 1:
+
+    def squares():
+        for r in range(KR):
+            if r not in seen:
+                seen.add(r)
+                take_bytes(gb[r], gsem.at[r])
+        acc = jnp.zeros((8, 128), jnp.float32)
+        for r in range(KR):
+            acc = square_tile(r, acc)
+        sq_own[...] = acc
+        for i in range(1, DPN):
+            send_square(sq_own, sq_in1.at[i], 0, dp_peer[i])
+
+    for k in range(-1, K):
+        if k >= 0:
+            second_hop(k)
+            if k + AHEAD < K:
+                first_hop(k + AHEAD)
+        if k == SUM_AT:
+            squares()
+        for n in range(4):
+            if k == LOAD_AT[n]:
+                loads[n].start()
+        if k == SUM_AT + 2:
             take_bytes(sq_in1.at[pl.ds(1, DPN - 1)], qr.at[0])
             mid = sq_own[...]
             for i in range(1, DPN):
@@ -256,13 +269,13 @@
             )
             out = (out * scale).astype(jnp.bfloat16)
             s3[k][:, :, pl.ds(n * TILE, TILE)] = out.reshape(MPN, ROWT, TILE)
-        for q in range(MPN - 1, 0, -1):
+        for q in ORDER3:
             send(s3[k].at[mp_peer[q][1]], r3[k].at[q], 2, k, mp_peer[q])
         r3[k][0] = s3[k][mp]
 
     def fourth_hop(k):
         take_bytes(s2[k].at[pl.ds(1, MPN - 1)], rsem.at[2, k])
-        for i in list(range(1, DPN)) + [0]:
+        for i in ORDER4:
             for n in (2 * i, 2 * i + 1):
                 piece = r3[k][tab[2, n]]
                 if i:

time: 79.5 us -> 78.2 us (0.984)
  Pallas kernels: 78.6 us -> 77.3 us
    pallas_call x1, Pallas kernels: 74.6 us -> 73.3 us  [per_device(): pl.pallas_call(kernel, name='shampoo', out_shape=tuple((pltpu.VMEM(*o) fo...]
where the time goes in v4:
time: 78.2 us; the launch traced here: 77.9 us
  Pallas kernels  77.3 us (99%)
    pallas_call x1, Pallas kernels, per_device(): pl.pallas_call(kernel, name='shampoo', out_shape=tuple((pltpu.VMEM(*o) fo...  73.3 us
    pallas_call x1, Pallas kernels, per_device(): pl.pallas_call(move, name='move', out_shape=tuple((jax.ShapeDtypeStruct(*...  4.02 us

profile of v4, /device:TPU:0, one launch (start us, length us, event | category | flops | bytes accessed | tf_op | source)
XLA Modules:
  0.0 77.9 jit_solution(2952389787067763028)
XLA Ops:
  0.6 73.3 %shampoo.1 = (f32[1024,1024]{1,0:T(8,128)S(1)}, f32[1024,1024]{1,0:T(8,128)S(1)}, bf16[64,16384]{1,0:T(8,128)(2,1)S(1)}) custom-call(s32[1,128]{1,0:T(1,128)} %bitcast.11, bf16[64,16384]{1,0:T(8,128)(2,1)} %grad.1, f32[1024,1024]{1,0:T(8,128)} %bitcast.7, f32[1024,1024]{1,0:T(8,128)} %bitcast.8, bf16[2,8,4,16,1024]{4,3,2,1,0:T(8,128)(2,1)} %bitcast.9, ...), custom_call_target="tpu_custom_call" | custom-call | tf_op jit(solution)/shard_map/shampoo/pallas_call | solution.py:366
  73.9 4.0 %move.1 = (f32[1024,1024]{1,0:T(8,128)}, f32[1024,1024]{1,0:T(8,128)}, bf16[64,16384]{1,0:T(8,128)(2,1)}) custom-call(f32[1024,1024]{1,0:T(8,128)S(1)} %get-tuple-element.9.refs_0_, f32[1024,1024]{1,0:T(8,128)S(1)} %get-tuple-element.10.refs_1_, bf16[64,16384]{1,0:T(8,128)(2,1)S(1)} %get-tuple-element.11.refs_2_), custom_call_target="tpu_custom_call" | custom-call | tf_op jit(solution)/shard_map/move/pallas_call | solution.py:406

commit v5 on v4

--- a/solution.py
+++ b/solution.py
@@ -16,7 +16,7 @@
 KR = SHARD // ROWT
 CHUNKS = [(row, col, 512) for row in range(4) for col in (0, 512)]
 K = len(CHUNKS)
-AHEAD = 3
+WINDOW = ((0, 1), (2, 3), (4, 5), (6,), (7,))
 BEHIND = 3
 TILE = 256
 ORDER1 = (1, 2, 3, 4, 5, 6, 7, 0)
@@ -180,7 +180,7 @@
             device_id_type=MESH,
         ).start()
 
-    for k in range(min(AHEAD, K)):
+    for k in WINDOW[0]:
         if k == 1:
             for r in range(1, KR):
                 load_grad(r)
@@ -207,8 +207,8 @@
     for k in range(-1, K):
         if k >= 0:
             second_hop(k)
-            if k + AHEAD < K:
-                first_hop(k + AHEAD)
+            for later in WINDOW[k + 1] if k + 1 < len(WINDOW) else ():
+                first_hop(later)
         if k == SUM_AT:
             squares()
         for n in range(4):

time: 78.2 us -> 77.7 us (level)
  no operation moved by 1% of the time
where the time goes in v5:
time: 77.7 us; the launch traced here: 77.4 us
  Pallas kernels  76.8 us (99%)
    pallas_call x1, Pallas kernels, per_device(): pl.pallas_call(kernel, name='shampoo', out_shape=tuple((pltpu.VMEM(*o) fo...  72.8 us
    pallas_call x1, Pallas kernels, per_device(): pl.pallas_call(move, name='move', out_shape=tuple((jax.ShapeDtypeStruct(*...  4.02 us

profile of v5, /device:TPU:0, one launch (start us, length us, event | category | flops | bytes accessed | tf_op | source)
XLA Modules:
  0.0 77.4 jit_solution(814329400442555309)
XLA Ops:
  0.6 72.8 %shampoo.1 = (f32[1024,1024]{1,0:T(8,128)S(1)}, f32[1024,1024]{1,0:T(8,128)S(1)}, bf16[64,16384]{1,0:T(8,128)(2,1)S(1)}) custom-call(s32[1,128]{1,0:T(1,128)} %bitcast.11, bf16[64,16384]{1,0:T(8,128)(2,1)} %grad.1, f32[1024,1024]{1,0:T(8,128)} %bitcast.7, f32[1024,1024]{1,0:T(8,128)} %bitcast.8, bf16[2,8,4,16,1024]{4,3,2,1,0:T(8,128)(2,1)} %bitcast.9, ...), custom_call_target="tpu_custom_call" | custom-call | tf_op jit(solution)/shard_map/shampoo/pallas_call | solution.py:366
  73.4 4.0 %move.1 = (f32[1024,1024]{1,0:T(8,128)}, f32[1024,1024]{1,0:T(8,128)}, bf16[64,16384]{1,0:T(8,128)(2,1)}) custom-call(f32[1024,1024]{1,0:T(8,128)S(1)} %get-tuple-element.9.refs_0_, f32[1024,1024]{1,0:T(8,128)S(1)} %get-tuple-element.10.refs_1_, bf16[64,16384]{1,0:T(8,128)(2,1)S(1)} %get-tuple-element.11.refs_2_), custom_call_target="tpu_custom_call" | custom-call | tf_op jit(solution)/shard_map/move/pallas_call | solution.py:406
